TPU v7x, 32 devices: a whole 2x2x4 slice. The times are simulated.
32 devices in a mesh: peer: 8 (over z, y), grp: 4 (over x, core).
Axes of the slice: x: 2, y: 2, z: 4, core: 2. Of those that a mesh axis runs over, the one named last changes fastest.
Arguments:
- tokens: bfloat16 [4096, 2048], P(('peer', 'grp')), may hold values from -6 to 6
- cotangent: bfloat16 [4096, 2048], P(('peer', 'grp')), may hold values from -6 to 6
- expert_ids: int32 [4096, 4], P(('peer', 'grp')), may hold values from 0 to 31, all different within a row; in each aligned block of 128 rows (0 to 127, 128 to 255, ...) at most 32 rows name the same one
- route_prob: float32 [4096, 4], P(('peer', 'grp')), may hold values from 0.1 to 1
- w_gate: bfloat16 [8, 2048, 704], P('peer', None, 'grp'), may hold values from -0.125 to 0.125
- w_up: bfloat16 [8, 2048, 704], P('peer', None, 'grp'), may hold values from -0.125 to 0.125
- w_down: bfloat16 [8, 704, 2048], P('peer', 'grp'), may hold values from -0.21875 to 0.21875
- student_logits: bfloat16 [8, 8, 151936], P('peer', None, 'grp'), may hold values from -24 to 252
- stale_logits: bfloat16 [8, 8, 151936], P('peer', None, 'grp'), may hold values from -24 to 252
- labels: int32 [8, 8], P('peer'), may hold values from 0 to 151935
Outputs:
- layer_out: bfloat16 [4096, 2048], P(('peer', 'grp'))
- input_grad: bfloat16 [4096, 2048], P(('peer', 'grp'))
- prob_grad: float32 [4096, 4], P(('peer', 'grp'))
- distill_loss: float32 [8, 8], P('peer')
- logit_grad: bfloat16 [8, 8, 151936], P('peer', None, 'grp')
Inputs may be any that keep to these rules, and one draw needn't show every extreme that they name: `expert_ids`: each row names 4 different experts; the rows of one device name any one expert at most 32 times.
All inputs are finite; a program needn't handle non-finite values.
Results may differ from a plain program's by a relative error of at most 0.0064.
Values may be sent and summed in bfloat16 or wider, within the bound.
No kernel may reach another device: no remote copies, remote signals or barrier semaphores. Data moves between devices by JAX's collectives and lax.ppermute only.
A program may use at most 64 MiB of HBM per device.

v0:
```python
import jax
import jax.numpy as jnp
from jax import lax
from jax.sharding import PartitionSpec as P

PIECES = 4
CAP = 32


def joined(value, axis, combine):
    everything = jax.tree.map(lambda part: lax.all_gather(part, axis), value)
    leading = jax.tree.map(lambda part: part[0], everything)

    def lap(k, so_far):
        return combine(so_far, jax.tree.map(lambda part: part[k], everything))

    return lax.fori_loop(1, lax.axis_size(axis), lap, leading)


def from_behind(value, axis, steps):
    count = lax.axis_size(axis)
    pairs = [(source, (source + steps) % count) for source in range(count)]
    return lax.ppermute(value, axis, pairs)


def slot_tables(expert_ids, n_window, capacity):
    window_iota = lax.broadcasted_iota(jnp.int32, (1, 1, n_window), 2)
    member = jnp.sum((expert_ids[:, :, None] == window_iota).astype(jnp.int32), axis=1)
    position = jnp.cumsum(member, axis=0) - member
    slot_iota = lax.broadcasted_iota(jnp.int32, (1, capacity, 1), 1)
    select = (position.T[:, None, :] == slot_iota) & (member.T[:, None, :] > 0)
    return (position, select)


def forward_piece(slot_rows, gate_cols, up_cols, down_rows):
    gate_act = jnp.dot(slot_rows, gate_cols, preferred_element_type=jnp.float32)
    up_act = jnp.dot(slot_rows, up_cols, preferred_element_type=jnp.float32)
    hidden = (gate_act * jax.nn.sigmoid(gate_act) * up_act).astype(jnp.bfloat16)
    piece_out = jnp.dot(hidden, down_rows, preferred_element_type=jnp.float32).astype(jnp.bfloat16)
    return (piece_out, gate_act, up_act)


def backward_piece(scaled_rows, gate_act, up_act, gate_cols, up_cols, down_rows):
    contract = (((1,), (1,)), ((), ()))
    grad_hidden = lax.dot_general(
        scaled_rows, down_rows, contract, preferred_element_type=jnp.float32
    )
    sigmoid_gate = jax.nn.sigmoid(gate_act)
    grad_gate = (
        grad_hidden * up_act * sigmoid_gate * (1.0 + gate_act * (1.0 - sigmoid_gate))
    ).astype(jnp.bfloat16)
    grad_up = (grad_hidden * gate_act * sigmoid_gate).astype(jnp.bfloat16)
    piece_grad = lax.dot_general(grad_gate, gate_cols, contract, preferred_element_type=jnp.float32)
    piece_grad = piece_grad + lax.dot_general(
        grad_up, up_cols, contract, preferred_element_type=jnp.float32
    )
    return piece_grad.astype(jnp.bfloat16)


def join_stats(first_side, second_side):
    max_one, sum_one, tmax_one, tsum_one, cross_one, label_one = first_side
    max_two, sum_two, tmax_two, tsum_two, cross_two, label_two = second_side
    max_both = jnp.maximum(max_one, max_two)
    tmax_both = jnp.maximum(tmax_one, tmax_two)
    scale_one = jnp.exp(tmax_one - tmax_both)
    scale_two = jnp.exp(tmax_two - tmax_both)
    sum_both = sum_one * jnp.exp(max_one - max_both) + sum_two * jnp.exp(max_two - max_both)
    tsum_both = tsum_one * scale_one + tsum_two * scale_two
    cross_both = cross_one * scale_one + cross_two * scale_two
    return (max_both, sum_both, tmax_both, tsum_both, cross_both, label_one + label_two)


def distill(student_logits, teacher_now, labels):
    student = student_logits[0].astype(jnp.float32)
    teacher = teacher_now[0].astype(jnp.float32)
    shard_width = student.shape[1]
    vocab_ids = lax.axis_index("grp") * shard_width + lax.broadcasted_iota(
        jnp.int32, student.shape, 1
    )
    label_hit = vocab_ids == labels[0][:, None]
    label_logit = jnp.sum(jnp.where(label_hit, student, 0.0), axis=1)
    local_smax = jnp.max(student, axis=1)
    local_tmax = jnp.max(teacher, axis=1)
    student_exp = jnp.sum(jnp.exp(student - local_smax[:, None]), axis=1)
    teacher_exp = jnp.exp(teacher - local_tmax[:, None])
    teacher_sum = jnp.sum(teacher_exp, axis=1)
    cross_sum = jnp.sum(teacher_exp * (teacher - student), axis=1)
    max_student, student_sum, max_teacher, teacher_sum, cross_sum, label_logit = joined(
        (local_smax, student_exp, local_tmax, teacher_sum, cross_sum, label_logit),
        "grp",
        join_stats,
    )
    lse_student = max_student + jnp.log(student_sum)
    lse_teacher = max_teacher + jnp.log(teacher_sum)
    distill_loss = 2.0 * lse_student - label_logit + cross_sum / teacher_sum - lse_teacher
    teacher_prob = jnp.exp(teacher - lse_teacher[:, None])
    logit_grad = (
        2.0 * jnp.exp(student - lse_student[:, None]) - label_hit.astype(jnp.float32) - teacher_prob
    ).astype(jnp.bfloat16)
    return (distill_loss[None], logit_grad[None])


def body(
    tokens,
    cotangent,
    expert_ids,
    route_prob,
    w_gate,
    w_up,
    w_down,
    student_logits,
    stale_logits,
    labels,
):
    group_size = lax.axis_size("grp")
    n_window = group_size // PIECES
    gate_cols = w_gate[0]
    up_cols = w_up[0]
    down_rows = w_down[0]
    model_width = tokens.shape[1]
    half_cap = CAP // 2
    position, select = slot_tables(expert_ids, n_window, CAP)
    select_bf = select.astype(jnp.bfloat16)
    window_iota = lax.broadcasted_iota(jnp.int32, (1, 1, n_window), 2)
    token_prob = jnp.sum(
        route_prob[:, :, None] * (expert_ids[:, :, None] == window_iota).astype(jnp.float32), axis=1
    )
    slot_prob = jnp.einsum(
        "ect,te->ec", select.astype(jnp.float32), token_prob, precision=lax.Precision.HIGHEST
    )
    slot_rows = jnp.einsum(
        "ect,td->ecd", select_bf, tokens, preferred_element_type=jnp.float32
    ).astype(jnp.bfloat16)
    slot_cot = jnp.einsum("ect,td->ecd", select_bf, cotangent, preferred_element_type=jnp.float32)
    slot_scaled = (slot_prob[:, :, None] * slot_cot).astype(jnp.bfloat16)
    send_rows = jnp.repeat(slot_rows, PIECES, axis=0).reshape(group_size, 2, half_cap, model_width)
    send_scaled = jnp.repeat(slot_scaled, PIECES, axis=0).reshape(
        group_size, 2, half_cap, model_width
    )
    recv_rows = lax.all_to_all(send_rows, "grp", split_axis=0, concat_axis=0, tiled=True)
    recv_scaled = lax.all_to_all(send_scaled, "grp", split_axis=0, concat_axis=0, tiled=True)
    item_count = recv_rows.shape[1]
    flat_rows = recv_rows.reshape(-1, model_width)
    flat_scaled = recv_scaled.reshape(-1, model_width)
    piece_out, gate_act, up_act = forward_piece(flat_rows, gate_cols, up_cols, down_rows)
    piece_out = piece_out.reshape(group_size, item_count, half_cap, model_width)
    piece_grad = backward_piece(flat_scaled, gate_act, up_act, gate_cols, up_cols, down_rows)
    piece_grad = piece_grad.reshape(group_size, item_count, half_cap, model_width)
    back_out = lax.all_to_all(piece_out, "grp", split_axis=0, concat_axis=0, tiled=True)
    back_grad = lax.all_to_all(piece_grad, "grp", split_axis=0, concat_axis=0, tiled=True)
    back_out, back_grad = (back_out, back_grad)
    expert_out = jnp.sum(
        back_out.astype(jnp.float32).reshape(n_window, PIECES, CAP, model_width), axis=1
    )
    expert_grad = jnp.sum(
        back_grad.astype(jnp.float32).reshape(n_window, PIECES, CAP, model_width), axis=1
    )
    in_window = expert_ids < n_window
    safe_ids = jnp.where(in_window, expert_ids, 0)
    slot_index = jnp.take_along_axis(position, safe_ids, axis=1)
    flat_index = safe_ids * CAP + slot_index
    out_rows = jnp.where(
        in_window[:, :, None],
        jnp.take(expert_out.reshape(-1, model_width), flat_index, axis=0),
        0.0,
    )
    grad_rows = jnp.where(
        in_window[:, :, None],
        jnp.take(expert_grad.reshape(-1, model_width), flat_index, axis=0),
        0.0,
    )
    layer_out = jnp.sum(route_prob[:, :, None] * out_rows, axis=1).astype(jnp.bfloat16)
    prob_grad = jnp.sum(cotangent.astype(jnp.float32)[:, None, :] * out_rows, axis=2)
    input_grad = jnp.sum(grad_rows, axis=1).astype(jnp.bfloat16)
    teacher_now = from_behind(stale_logits, "peer", 1)
    distill_loss, logit_grad = distill(student_logits, teacher_now, labels)
    return (layer_out, input_grad, prob_grad, distill_loss, logit_grad)


def solution(mesh):
    placed = (
        P(("peer", "grp"), None),
        P(("peer", "grp"), None),
        P(("peer", "grp"), None),
        P(("peer", "grp"), None),
        P("peer", None, "grp"),
        P("peer", None, "grp"),
        P("peer", "grp", None),
        P("peer", None, "grp"),
        P("peer", None, "grp"),
        P("peer", None),
    )
    return jax.shard_map(
        body,
        mesh=mesh,
        in_specs=placed,
        out_specs=(
            P(("peer", "grp"), None),
            P(("peer", "grp"), None),
            P(("peer", "grp"), None),
            P("peer", None),
            P("peer", None, "grp"),
        ),
        check_vma=False,
    )
```

profile of v0, /device:TPU:0, one launch (start us, length us, event | category | flops | bytes accessed | tf_op | source)
XLA Modules:
  0.0 88.1 jit_solution(13793682521302028346)
XLA Ops:
  0.6 3.0 %collective-permute-start = (bf16[1,8,37984]{2,1,0:T(8,128)(2,1)}, bf16[1,8,37984]{2,1,0:T(8,128)(2,1)S(1)}, u32[]{:S(2)}, u32[]{:S(2)}) collective-permute-start(bf16[1,8,37984]{2,1,0:T(8,128)(2,1)} %param.22), channel_id=1, source_target_pairs={{0,4},{4,8},{8,12},{12,16},{16,20},{20,24},{24,28},{28,0},{1,5},{5... | collective-permute-start | bytes 1823240 | tf_op jit(solution)/shard_map/ppermute | solution.py:23
  3.7 0.7 select_reduce_fusion
  4.9 1.2 %convolution_convert_fusion.1 = bf16[32,2048]{1,0:T(8,128)(2,1)S(1)} fusion(bf16[128,2048]{1,0:T(8,128)(2,1)} %param.14, s32[128]{0:T(128)S(1)} %sub.111, pred[128]{0:T(512)(128)(4,1)S(1)} %broadcast_compare_fusion.2), kind=kOutput, calls=%fused_computation.36 | convolution fusion | flops 16850944 | bytes 656000 | tf_op jit(solution)/shard_map/ect,td->ecd/dot_general | solution.py:131
  6.1 0.8 broadcast_in_dim.63
  7.0 3.5 %all-to-all-start = ((bf16[4,2,16,2048]{3,2,1,0:T(8,128)(2,1)}), bf16[4,2,16,2048]{3,2,1,0:T(8,128)(2,1)S(1)}, u32[]{:S(2)}, u32[]{:S(2)}) async-start(bf16[4,2,16,2048]{3,2,1,0:T(8,128)(2,1)} %broadcast_in_dim.63), calls=%async_computation | async-start | bytes 1048576 | tf_op jit(solution)/shard_map/all_to_all | solution.py:140
  10.8 3.4 %gather_fusion = s32[512]{0:T(512)S(1)} fusion(s32[128,1]{1,0:T(8,128)S(1)} %get-tuple-element.386, s32[512]{0:T(512)S(1)} %reshape.285), kind=kCustom, calls=%fused_computation.2 | custom fusion | bytes 8192 | tf_op jit(solution)/shard_map/jit(take_along_axis)/gather | solution.py:160
  14.6 0.4 reduce_max.36
  15.1 0.6 dynamic-slice
  16.4 0.7 copy.40
  17.5 1.2 %convert_element_type.89 = f32[128,2048]{1,0:T(8,128)} convert(bf16[128,2048]{1,0:T(8,128)(2,1)S(1)} %copy-done.5) | non-fusion elementwise | flops 262144 | bytes 1572864 | tf_op jit(solution)/shard_map/convert_element_type | solution.py:173
  19.2 0.8 broadcast_in_dim.67
  20.1 4.3 %all-to-all-start.2 = ((bf16[4,2,16,2048]{3,2,1,0:T(8,128)(2,1)}), bf16[4,2,16,2048]{3,2,1,0:T(8,128)(2,1)}, u32[]{:S(2)}, u32[]{:S(2)}) async-start(bf16[4,2,16,2048]{3,2,1,0:T(8,128)(2,1)} %broadcast_in_dim.67), calls=%async_computation.2 | async-start | bytes 1048576 | tf_op jit(solution)/shard_map/all_to_all | solution.py:141
  24.3 0.4 fusion.43
  24.7 1.0 %fusion.39 = f32[128,176]{0,1:T(8,128)} fusion(bf16[128,2048]{1,0:T(8,128)(2,1)S(1)} %bitcast.127, bf16[1,2048,176]{1,2,0:T(8,128)(2,1)S(1)} %copy-done.3), kind=kOutput, calls=%fused_computation.65 | convolution fusion | flops 92274688 | bytes 1335296 | tf_op jit(solution)/shard_map/dot_general | solution.py:37
  25.8 7.4 %all-to-all-done.2 = bf16[4,2,16,2048]{3,2,1,0:T(8,128)(2,1)} async-done(((bf16[4,2,16,2048]{3,2,1,0:T(8,128)(2,1)}), bf16[4,2,16,2048]{3,2,1,0:T(8,128)(2,1)}, u32[]{:S(2)}, u32[]{:S(2)}) %all-to-all-start.2) | async-done | bytes 524320 | tf_op jit(solution)/shard_map/all_to_all | solution.py:141
  33.2 1.6 %fusion.35 = f32[128,176]{0,1:T(8,128)S(1)} fusion(bf16[128,2048]{1,0:T(8,128)(2,1)} %bitcast.18, bf16[1,176,2048]{2,1,0:T(8,128)(2,1)} %param.20), kind=kOutput, calls=%fused_computation.61 | convolution fusion | flops 92274688 | bytes 1335296 | tf_op jit(solution)/shard_map/dot_general | solution.py:45
  34.8 0.4 fusion.41
  35.2 1.1 %fusion.16 = bf16[128,2048]{1,0:T(8,128)(2,1)} fusion(f32[128,2048]{1,0:T(8,128)S(1)} %fusion.41, bf16[1,2048,176]{1,2,0:T(8,128)(2,1)S(1)} %copy-done.3, f32[128,176]{0,1:T(8,128)S(1)} %fusion.35, f32[128,176]{0,1:T(8,128)S(1)} %fusion.43), kind=kOutput, calls=%fused_computation.32 | convolution fusion | flops 92934144 | bytes 2473984 | tf_op jit(solution)/shard_map/dot_general | solution.py:54
  36.4 3.6 %all-to-all-start.3 = ((bf16[4,2,16,2048]{3,2,1,0:T(8,128)(2,1)}), bf16[4,2,16,2048]{3,2,1,0:T(8,128)(2,1)S(1)}, u32[]{:S(2)}, u32[]{:S(2)}) async-start(bf16[4,2,16,2048]{3,2,1,0:T(8,128)(2,1)} %bitcast.19), calls=%async_computation.3 | async-start | bytes 1048576 | tf_op jit(solution)/shard_map/all_to_all | solution.py:150
  40.0 2.0 %convolution_convert_fusion = bf16[128,2048]{1,0:T(8,128)(2,1)} fusion(bf16[1,176,2048]{2,1,0:T(8,128)(2,1)S(1)} %copy-done.4, f32[128,176]{0,1:T(8,128)} %fusion.39, f32[128,176]{0,1:T(8,128)S(1)} %fusion.43), kind=kOutput, calls=%fused_computation.33 | convolution fusion | flops 92672000 | bytes 1425408 | tf_op jit(solution)/shard_map/dot_general | solution.py:39
  42.0 0.4 reduce_max.40
  42.6 1.2 %fusion.33 = (f32[8]{0:T(128)S(1)}, f32[8]{0:T(128)S(1)}, f32[8]{0:T(128)S(1)}, f32[8]{0:T(128)S(1)}) fusion(bf16[1,8,37984]{2,1,0:T(8,128)(2,1)S(1)} %collective-permute-done, bf16[1,8,37984]{2,1,0:T(8,128)(2,1)S(1)} %copy-done.1, f32[8]{0:T(128)S(1)} %reduce_max.45, s32[8]{0:T(128)S(1)} %bitcast.137, s32[37984]{0:T(1024)S(1)} %iota_add_fusion, ...), kind=kLoop, calls=%fused_computation.56 | loop fusion | flops 3646432 | bytes 1367648 | tf_op jit(solution)/shard_map/reduce_sum | solution.py:87
  44.6 7.3 %all-reduce.6 = (f32[32]{0:T(128)S(1)}, f32[32]{0:T(128)S(1)}, f32[32]{0:T(128)S(1)}, f32[32]{0:T(128)S(1)}, f32[32]{0:T(128)S(1)}, /*index=5*/f32[32]{0:T(128)S(1)}) all-reduce(f32[32]{0:T(128)S(1)} %convert_dynamic-update-slice_fusion.1, f32[32]{0:T(128)S(1)} %dynamic-update-slice.1, ...), channel_id=2, replica_groups=mesh['peer'=8,'grp'=4] {'grp'}, use_global_device_ids=true, to_apply=%add | all-reduce | flops 192 | bytes 1536
  52.7 0.5 subtract_bitcast_fusion
  53.2 3.7 %all-to-all-start.1 = ((bf16[4,2,16,2048]{3,2,1,0:T(8,128)(2,1)}), bf16[4,2,16,2048]{3,2,1,0:T(8,128)(2,1)S(1)}, u32[]{:S(2)}, u32[]{:S(2)}) async-start(bf16[4,2,16,2048]{3,2,1,0:T(8,128)(2,1)} %bitcast.128), calls=%async_computation.1 | async-start | bytes 1048576 | tf_op jit(solution)/shard_map/all_to_all | solution.py:149
  56.9 1.4 %fusion.29 = bf16[1,8,37984]{2,1,0:T(8,128)(2,1)} fusion(bf16[1,8,37984]{2,1,0:T(8,128)(2,1)S(1)} %copy-done.1, bf16[1,8,37984]{2,1,0:T(8,128)(2,1)S(1)} %collective-permute-done, f32[8]{0:T(128)S(1)} %get-tuple-element.380, s32[37984]{0:T(1024)S(1)} %iota_add_fusion, f32[8]{0:T(128)S(1)} %get-tuple-element.379, s32[8]{0:T(128)S(1)} %bitcast.138), kind=kLoop, calls=%fused_computation.52 | loop fusion | flops 3038720 | bytes 1975264 | tf_op jit(solution)/shard_map/convert_element_type | solution.py:99
  58.4 3.6 %gather_fusion.2 = f32[512,2048]{1,0:T(8,128)} fusion(f32[32,2048]{1,0:T(8,128)S(1)} %bitcast.125, s32[1024]{0:T(1024)S(1)} %pad_clamp_fusion), kind=kCustom, calls=%fused_computation.1.clone | custom fusion | bytes 8390656 | tf_op jit(solution)/shard_map/jit(_take)/gather | solution.py:169
  62.0 5.2 %reshape.355 = f32[128,4,2048]{2,1,0:T(4,128)} reshape(f32[512,2048]{1,0:T(8,128)} %gather_fusion.2) | data formatting | bytes 8388608 | tf_op jit(solution)/shard_map/jit(_take)/gather | solution.py:169
  67.3 3.6 %gather_fusion.1 = f32[512,2048]{1,0:T(8,128)} fusion(f32[32,2048]{1,0:T(8,128)S(1)} %bitcast.124, s32[1024]{0:T(1024)S(1)} %pad_clamp_fusion), kind=kCustom, calls=%fused_computation.clone | custom fusion | bytes 8390656 | tf_op jit(solution)/shard_map/jit(_take)/gather | solution.py:164
  70.9 5.3 %reshape.351 = f32[128,4,2048]{2,1,0:T(4,128)} reshape(f32[512,2048]{1,0:T(8,128)} %gather_fusion.1) | data formatting | bytes 8388608 | tf_op jit(solution)/shard_map/jit(_take)/gather | solution.py:164
  76.1 11.4 %multiply_reduce_fusion = (f32[128,4]{1,0:T(8,128)S(1)}, bf16[128,2048]{1,0:T(8,128)(2,1)}, bf16[128,2048]{1,0:T(8,128)(2,1)}) fusion(f32[128,4,2048]{2,1,0:T(4,128)} %reshape.351, f32[128,2048]{1,0:T(8,128)S(1)} %copy-done.2, pred[128,4]{1,0:T(8,128)(4,1)S(1)} %copy.46, pred[128,4]{1,0:T(8,128)(4,1)S(1)} %copy.41, f32[128,4]{1,0:T(8,128)S(1)} %copy-done.7, ...), kind=kLoop, calls=%fused_computation.29 | loop fusion | flops 8912384 | bytes 10490880 | tf_op jit(solution)/shard_map/reduce_sum | solution.py:173
  87.5 0.7 copy.50
  (83 shorter events, 4.2 us)
Async XLA Ops:
  0.6 23.7 %copy-start = (bf16[1,2048,176]{1,2,0:T(8,128)(2,1)S(1)}, bf16[1,2048,176]{1,2,0:T(8,128)(2,1)}, u32[]{:S(2)}) copy-start(bf16[1,2048,176]{1,2,0:T(8,128)(2,1)} %param.18) | copy-start | bytes 2162692
  0.6 41.4 %collective-permute-start = (bf16[1,8,37984]{2,1,0:T(8,128)(2,1)}, bf16[1,8,37984]{2,1,0:T(8,128)(2,1)S(1)}, u32[]{:S(2)}, u32[]{:S(2)}) collective-permute-start(bf16[1,8,37984]{2,1,0:T(8,128)(2,1)} %param.22), channel_id=1, source_target_pairs={{0,4},{4,8},{8,12},{12,16},{16,20},{20,24},{24,28},{28,0},{1,5},{5... | collective-permute-start | bytes 1823240 | tf_op jit(solution)/shard_map/ppermute | solution.py:23
  4.8 5.6 %copy-start.8 = (s32[128,4]{0,1:T(4,128)S(1)}, s32[128,4]{0,1:T(4,128)}, u32[]{:S(2)}) copy-start(s32[128,4]{0,1:T(4,128)} %param.16) | copy-start | bytes 6148
  7.0 12.3 %all-to-all-start = ((bf16[4,2,16,2048]{3,2,1,0:T(8,128)(2,1)}), bf16[4,2,16,2048]{3,2,1,0:T(8,128)(2,1)S(1)}, u32[]{:S(2)}, u32[]{:S(2)}) async-start(bf16[4,2,16,2048]{3,2,1,0:T(8,128)(2,1)} %broadcast_in_dim.63), calls=%async_computation | async-start | bytes 1048576 | tf_op jit(solution)/shard_map/all_to_all | solution.py:140
  10.7 3.9 %copy-start.1 = (bf16[1,8,37984]{2,1,0:T(8,128)(2,1)S(1)}, bf16[1,8,37984]{2,1,0:T(8,128)(2,1)}, u32[]{:S(2)}) copy-start(bf16[1,8,37984]{2,1,0:T(8,128)(2,1)} %param.21) | copy-start | bytes 1823236
  10.7 4.3 %copy-start.11 = (u32[32]{0:T(128)S(1)}, u32[32]{0:T(128)}, u32[]{:S(2)}) copy-start(u32[32]{0:T(128)} %constant.107) | copy-start | bytes 388
  10.7 5.7 %copy-start.9 = (f32[128,4]{0,1:T(4,128)S(1)}, f32[128,4]{0,1:T(4,128)}, u32[]{:S(2)}) copy-start(f32[128,4]{0,1:T(4,128)} %param.17) | copy-start | bytes 6148
  14.2 3.3 %copy-start.5 = (bf16[128,2048]{1,0:T(8,128)(2,1)S(1)}, bf16[128,2048]{1,0:T(8,128)(2,1)}, u32[]{:S(2)}) copy-start(bf16[128,2048]{1,0:T(8,128)(2,1)} %param.15) | copy-start | bytes 1572868
  20.1 4.7 %copy-start.3 = (bf16[1,2048,176]{1,2,0:T(8,128)(2,1)S(1)}, bf16[1,2048,176]{1,2,0:T(8,128)(2,1)}, u32[]{:S(2)}) copy-start(bf16[1,2048,176]{1,2,0:T(8,128)(2,1)} %param.19) | copy-start | bytes 2162692
  20.1 13.1 %all-to-all-start.2 = ((bf16[4,2,16,2048]{3,2,1,0:T(8,128)(2,1)}), bf16[4,2,16,2048]{3,2,1,0:T(8,128)(2,1)}, u32[]{:S(2)}, u32[]{:S(2)}) async-start(bf16[4,2,16,2048]{3,2,1,0:T(8,128)(2,1)} %broadcast_in_dim.67), calls=%async_computation.2 | async-start | bytes 1048576 | tf_op jit(solution)/shard_map/all_to_all | solution.py:141
  25.8 9.1 %copy-start.6 = (f32[128,176]{0,1:T(8,128)S(1)}, f32[128,176]{0,1:T(8,128)}, u32[]{:S(2)}) copy-start(f32[128,176]{0,1:T(8,128)} %fusion.39) | copy-start | bytes 270340
  36.4 3.6 %copy-start.4 = (bf16[1,176,2048]{2,1,0:T(8,128)(2,1)S(1)}, bf16[1,176,2048]{2,1,0:T(8,128)(2,1)}, u32[]{:S(2)}) copy-start(bf16[1,176,2048]{2,1,0:T(8,128)(2,1)} %param.20) | copy-start | bytes 2162692
  36.4 16.9 %all-to-all-start.3 = ((bf16[4,2,16,2048]{3,2,1,0:T(8,128)(2,1)}), bf16[4,2,16,2048]{3,2,1,0:T(8,128)(2,1)S(1)}, u32[]{:S(2)}, u32[]{:S(2)}) async-start(bf16[4,2,16,2048]{3,2,1,0:T(8,128)(2,1)} %bitcast.19), calls=%async_computation.3 | async-start | bytes 1048576 | tf_op jit(solution)/shard_map/all_to_all | solution.py:150
  40.0 2.6 %copy-start.10 = (s32[1,8]{1,0:T(1,128)S(1)}, s32[1,8]{1,0:T(1,128)}, u32[]{:S(2)}) copy-start(s32[1,8]{1,0:T(1,128)} %param.23) | copy-start | bytes 100
  53.2 14.0 %all-to-all-start.1 = ((bf16[4,2,16,2048]{3,2,1,0:T(8,128)(2,1)}), bf16[4,2,16,2048]{3,2,1,0:T(8,128)(2,1)S(1)}, u32[]{:S(2)}, u32[]{:S(2)}) async-start(bf16[4,2,16,2048]{3,2,1,0:T(8,128)(2,1)} %bitcast.128), calls=%async_computation.1 | async-start | bytes 1048576 | tf_op jit(solution)/shard_map/all_to_all | solution.py:149
  70.9 5.3 %copy-start.2 = (f32[128,2048]{1,0:T(8,128)S(1)}, f32[128,2048]{1,0:T(8,128)}, u32[]{:S(2)}) copy-start(f32[128,2048]{1,0:T(8,128)} %convert_element_type.89) | copy-start | bytes 3145732
  70.9 5.3 %copy-start.7 = (f32[128,4]{1,0:T(8,128)S(1)}, f32[128,4]{1,0:T(8,128)}, u32[]{:S(2)}) copy-start(f32[128,4]{1,0:T(8,128)} %copy.40) | copy-start | bytes 6148
where the time goes:
time: 88.8 us; the launch traced here: 88.1 us
  local copies, waits for them, and re-layouts  27.1 us (31%)
  other arithmetic  18.1 us (20%)
  starting transfers between devices  18 us (20%)
  matrix products  8.18 us (9%)
  waiting for transfers between devices  7.67 us (9%)
  blocking collectives  7.33 us (8%)
  between operations  1.6 us (2%)
    reduce_sum x1, other arithmetic, body(): jnp.sum(cotangent.astype(jnp.float32)[:, None, :] * out_rows, axis=2)  11.4 us
    gather x2, local copies, waits for them, and re-layouts, body(): jnp.take(expert_out.reshape(-1, model_width), flat_index, axis=0)  8.83 us
    gather x2, local copies, waits for them, and re-layouts, body(): jnp.take(expert_grad.reshape(-1, model_width), flat_index, axis=0)  8.79 us
    all_to_all x1, waiting for transfers between devices, body(): lax.all_to_all(send_scaled, 'grp', split_axis=0, concat_axis=0, tiled=True)  7.41 us
    unnamed x1, blocking collectives  7.33 us
    all_to_all x1, starting transfers between devices, body(): lax.all_to_all(send_scaled, 'grp', split_axis=0, concat_axis=0, tiled=True)  4.26 us
    gather x5, local copies, waits for them, and re-layouts, body(): slot_index = jnp.take_along_axis(position, safe_ids, axis=1)  3.81 us
    all_to_all x1, starting transfers between devices, body(): lax.all_to_all(piece_out, 'grp', split_axis=0, concat_axis=0, tiled=True)  3.65 us
  transfers between devices with their start and end apart: 5, of which 2 were waited for; matrix products, arithmetic and copies ran while one was open for 37% of the time, Pallas kernels for 0%

commit v1 on v0

--- a/solution.py
+++ b/solution.py
@@ -5,6 +5,29 @@
 
 PIECES = 4
 CAP = 32
+
+
+def cut_along(x, dim, length):
+    before, after = (x.shape[:dim], x.shape[dim + 1 :])
+    return jnp.moveaxis(x.reshape(*before, length, -1, *after), dim, 0)
+
+
+def joined_along(parts, dim):
+    parts = jnp.moveaxis(parts, 0, dim)
+    lengths = parts.shape
+    return parts.reshape(*lengths[:dim], lengths[dim] * lengths[dim + 1], *lengths[dim + 2 :])
+
+
+def sent_to_each(x, axis, split_dim, concat_dim):
+    size, here = (lax.axis_size(axis), lax.axis_index(axis))
+    blocks = cut_along(x, split_dim, size)
+    out = blocks
+    for hop in range(1, size):
+        target, source = ((here + hop) % size, (here - hop) % size)
+        sent = lax.dynamic_index_in_dim(blocks, target, 0)
+        partner_block = lax.ppermute(sent, axis, [(i, (i + hop) % size) for i in range(size)])
+        out = lax.dynamic_update_slice_in_dim(out, partner_block, source, axis=0)
+    return joined_along(out, concat_dim)
 
 
 def joined(value, axis, combine):
@@ -138,7 +161,7 @@
         group_size, 2, half_cap, model_width
     )
     recv_rows = lax.all_to_all(send_rows, "grp", split_axis=0, concat_axis=0, tiled=True)
-    recv_scaled = lax.all_to_all(send_scaled, "grp", split_axis=0, concat_axis=0, tiled=True)
+    recv_scaled = sent_to_each(send_scaled, "grp", 0, 0)
     item_count = recv_rows.shape[1]
     flat_rows = recv_rows.reshape(-1, model_width)
     flat_scaled = recv_scaled.reshape(-1, model_width)

time: 88.8 us -> 82.5 us (0.929)
  waiting for transfers between devices: 7.67 us -> 0.02 us
  local copies, waits for them, and re-layouts: 27.1 us -> 29.7 us
  starting transfers between devices: 18 us -> 16.7 us
    all_to_all x1 -> x0, waiting for transfers between devices: 7.41 us -> none  [body(): lax.all_to_all(send_scaled, 'grp', split_axis=0, concat_axis=0, tiled=True)]
    ppermute x0 -> x3, starting transfers between devices: none -> 4.48 us  [sent_to_each(): lax.ppermute(sent, axis, [(i, (i + hop) % size) for i in range(size)])]
    all_to_all x1 -> x0, starting transfers between devices: 4.26 us -> none  [body(): lax.all_to_all(send_scaled, 'grp', split_axis=0, concat_axis=0, tiled=True)]
    dynamic_update_slice x0 -> x3, local copies, waits for them, and re-layouts: none -> 2.76 us  [sent_to_each(): out = lax.dynamic_update_slice_in_dim(out, partner_block, source, axis=0)]
    ppermute x1, starting transfers between devices: 3.05 us -> 1.52 us  [from_behind(): return lax.ppermute(value, axis, pairs)]
    dot_general x1, matrix products: 1.24 us -> 0.19 us  [body(): jnp.einsum('ect,td->ecd', select_bf, tokens, preferred_element_type=jnp.f...]
    dot_general x1, matrix products: 0.22 us -> 1.27 us  [body(): jnp.einsum('ect,td->ecd', select_bf, cotangent, preferred_element_type=jn...]
    unnamed x37 -> x41, local copies, waits for them, and re-layouts: 2.89 us -> 3.53 us
  transfers between devices with their start and end apart: 5 -> 7, of which waited for: 2 -> 0; matrix products, arithmetic and copies ran while one was open for 37% -> 39% of each run, Pallas kernels for 0% -> 0%
where the time goes in v1:
time: 82.5 us; the launch traced here: 81.9 us
  local copies, waits for them, and re-layouts  29.7 us (36%)
  other arithmetic  18.2 us (22%)
  starting transfers between devices  16.7 us (20%)
  matrix products  8.07 us (10%)
  blocking collectives  7.34 us (9%)
  between operations  1.67 us (2%)
    reduce_sum x1, other arithmetic, body(): jnp.sum(cotangent.astype(jnp.float32)[:, None, :] * out_rows, axis=2)  11.4 us
    gather x2, local copies, waits for them, and re-layouts, body(): jnp.take(expert_out.reshape(-1, model_width), flat_index, axis=0)  8.83 us
    gather x2, local copies, waits for them, and re-layouts, body(): jnp.take(expert_grad.reshape(-1, model_width), flat_index, axis=0)  8.79 us
    unnamed x1, blocking collectives  7.34 us
    ppermute x3, starting transfers between devices, sent_to_each(): lax.ppermute(sent, axis, [(i, (i + hop) % size) for i in range(size)])  4.48 us
    gather x5, local copies, waits for them, and re-layouts, body(): slot_index = jnp.take_along_axis(position, safe_ids, axis=1)  3.81 us
    all_to_all x1, starting transfers between devices, body(): lax.all_to_all(piece_out, 'grp', split_axis=0, concat_axis=0, tiled=True)  3.65 us
    all_to_all x1, starting transfers between devices, body(): lax.all_to_all(piece_grad, 'grp', split_axis=0, concat_axis=0, tiled=True)  3.6 us
  transfers between devices with their start and end apart: 7, of which 0 were waited for; matrix products, arithmetic and copies ran while one was open for 39% of the time, Pallas kernels for 0%

profile of v1, /device:TPU:0, one launch (start us, length us, event | category | flops | bytes accessed | tf_op | source)
XLA Modules:
  0.0 81.9 jit_solution(8830657055690544281)
XLA Ops:
  0.7 0.8 select_reduce_fusion
  2.0 1.3 %fusion.17 = bf16[32,2048]{1,0:T(8,128)(2,1)S(1)} fusion(bf16[128,2048]{1,0:T(8,128)(2,1)} %param.15, f32[32]{0:T(128)S(1)} %convolution_bitcast_fusion, s32[128]{0:T(128)S(1)} %sub.120, pred[128]{0:T(512)(128)(4,1)S(1)} %broadcast_compare_fusion.2), kind=kOutput, calls=%fused_computation.35 | convolution fusion | flops 16916480 | bytes 656128 | tf_op jit(solution)/shard_map/ect,td->ecd/dot_general | solution.py:157
  3.3 0.5 collective-permute-start
  3.9 2.6 %collective-permute-start.1 = (bf16[1,1,2,16,2048]{4,3,2,1,0:T(8,128)(2,1)S(1)}, bf16[1,1,2,16,2048]{4,3,2,1,0:T(8,128)(2,1)}, u32[]{:S(2)}, u32[]{:S(2)}) collective-permute-start(bf16[1,1,2,16,2048]{4,3,2,1,0:T(8,128)(2,1)S(1)} %bitcast.133), channel_id=1, source_target_pairs={{0,2},{1,3},{2,0},{3,1},{4,6},{5,7},{6,4},{7,5},{8,10},{9,11},{10,... | collective-permute-start | bytes 393224 | tf_op jit(solution)/shard_map/ppermute | solution.py:28
  6.4 1.4 %collective-permute-start.2 = (bf16[1,1,2,16,2048]{4,3,2,1,0:T(8,128)(2,1)S(1)}, bf16[1,1,2,16,2048]{4,3,2,1,0:T(8,128)(2,1)}, u32[]{:S(2)}, u32[]{:S(2)}) collective-permute-start(bf16[1,1,2,16,2048]{4,3,2,1,0:T(8,128)(2,1)S(1)} %bitcast.134), channel_id=1, source_target_pairs={{0,3},{1,0},{2,1},{3,2},{4,7},{5,4},{6,5},{7,6},{8,11},{9,8},{10,9... | collective-permute-start | bytes 393224 | tf_op jit(solution)/shard_map/ppermute | solution.py:28
  7.8 1.5 %collective-permute-start.3 = (bf16[1,8,37984]{2,1,0:T(8,128)(2,1)}, bf16[1,8,37984]{2,1,0:T(8,128)(2,1)S(1)}, u32[]{:S(2)}, u32[]{:S(2)}) collective-permute-start(bf16[1,8,37984]{2,1,0:T(8,128)(2,1)} %param.22), channel_id=1, source_target_pairs={{0,4},{4,8},{8,12},{12,16},{16,20},{20,24},{24,28},{28,0},{1,5},{5... | collective-permute-start | bytes 1823240 | tf_op jit(solution)/shard_map/ppermute | solution.py:46
  9.5 0.9 %broadcast_in_dim.65 = bf16[4,2,16,2048]{3,2,1,0:T(8,128)(2,1)} broadcast(bf16[2,16,2048]{2,1,0:T(8,128)(2,1)S(1)} %bitcast.131), dimensions={1,2,3} | broadcast | bytes 655360 | tf_op jit(solution)/shard_map/broadcast_in_dim | solution.py:159
  10.4 3.5 %all-to-all-start = ((bf16[4,2,16,2048]{3,2,1,0:T(8,128)(2,1)}), bf16[4,2,16,2048]{3,2,1,0:T(8,128)(2,1)S(1)}, u32[]{:S(2)}, u32[]{:S(2)}) async-start(bf16[4,2,16,2048]{3,2,1,0:T(8,128)(2,1)} %broadcast_in_dim.65), calls=%async_computation | async-start | bytes 1048576 | tf_op jit(solution)/shard_map/all_to_all | solution.py:163
  14.2 3.4 %gather_fusion = s32[512]{0:T(512)S(1)} fusion(s32[128,1]{1,0:T(8,128)S(1)} %get-tuple-element.386, s32[512]{0:T(512)S(1)} %reshape.287), kind=kCustom, calls=%fused_computation.2 | custom fusion | bytes 8192 | tf_op jit(solution)/shard_map/jit(take_along_axis)/gather | solution.py:183
  17.8 0.4 reduce_max.36
  18.3 0.6 dynamic-slice.3
  19.6 1.2 %convert_element_type.89 = f32[128,2048]{1,0:T(8,128)} convert(bf16[128,2048]{1,0:T(8,128)(2,1)S(1)} %copy-done.5) | non-fusion elementwise | flops 262144 | bytes 1572864 | tf_op jit(solution)/shard_map/convert_element_type | solution.py:196
  20.8 0.7 copy.40
  22.1 0.9 %constant_dynamic-update-slice_fusion.2 = bf16[4,1,2,16,2048]{4,3,2,1,0:T(8,128)(2,1)S(1)} fusion(bf16[4,1,2,16,2048]{4,3,2,1,0:T(8,128)(2,1)S(1)} %broadcast_in_dim.69, bf16[1,1,2,16,2048]{4,3,2,1,0:T(8,128)(2,1)} %collective-permute-done, s32[]{:T(128)S(6)} %select_n.84), kind=kLoop, calls=%fused_computation.98 | loop fusion | bytes 262148 | tf_op jit(solution)/shard_map/dynamic_update_slice | solution.py:29
  23.1 0.9 %constant_dynamic-update-slice_fusion.1 = bf16[4,1,2,16,2048]{4,3,2,1,0:T(8,128)(2,1)S(1)} fusion(bf16[4,1,2,16,2048]{4,3,2,1,0:T(8,128)(2,1)S(1)} %constant_dynamic-update-slice_fusion.2, bf16[1,1,2,16,2048]{4,3,2,1,0:T(8,128)(2,1)} %collective-permute-done.1, s32[]{:T(128)S(6)} %select_n.86), kind=kLoop, calls=%fused_computation.97 | loop fusion | bytes 262148 | tf_op jit(solution)/shard_map/dynamic_update_slice | solution.py:29
  24.0 0.9 %constant_dynamic-update-slice_fusion = bf16[4,1,2,16,2048]{4,3,2,1,0:T(8,128)(2,1)S(1)} fusion(bf16[4,1,2,16,2048]{4,3,2,1,0:T(8,128)(2,1)S(1)} %constant_dynamic-update-slice_fusion.1, bf16[1,1,2,16,2048]{4,3,2,1,0:T(8,128)(2,1)} %collective-permute-done.2, s32[]{:T(128)S(6)} %select_n.88), kind=kLoop, calls=%fused_computation.96 | loop fusion | bytes 262148 | tf_op jit(solution)/shard_map/dynamic_update_slice | solution.py:29
  24.9 2.2 %fusion.35 = f32[128,176]{0,1:T(8,128)} fusion(bf16[128,2048]{1,0:T(8,128)(2,1)S(1)} %bitcast.129, bf16[1,176,2048]{2,1,0:T(8,128)(2,1)} %param.20), kind=kOutput, calls=%fused_computation.61 | convolution fusion | flops 92274688 | bytes 1335296 | tf_op jit(solution)/shard_map/dot_general | solution.py:68
  27.9 0.6 copy-done.7
  28.9 1.1 %fusion.16 = bf16[128,2048]{1,0:T(8,128)(2,1)} fusion(f32[128,2048]{1,0:T(8,128)S(1)} %fusion.41, bf16[1,2048,176]{1,2,0:T(8,128)(2,1)S(1)} %copy-done.3, f32[128,176]{0,1:T(8,128)S(1)} %copy-done.6, f32[128,176]{0,1:T(8,128)S(1)} %fusion.43), kind=kOutput, calls=%fused_computation.32 | convolution fusion | flops 92934144 | bytes 2473984 | tf_op jit(solution)/shard_map/dot_general | solution.py:77
  30.1 3.6 %all-to-all-start.2 = ((bf16[4,2,16,2048]{3,2,1,0:T(8,128)(2,1)}), bf16[4,2,16,2048]{3,2,1,0:T(8,128)(2,1)S(1)}, u32[]{:S(2)}, u32[]{:S(2)}) async-start(bf16[4,2,16,2048]{3,2,1,0:T(8,128)(2,1)} %bitcast.20), calls=%async_computation.2 | async-start | bytes 1048576 | tf_op jit(solution)/shard_map/all_to_all | solution.py:173
  33.7 2.0 %convolution_convert_fusion = bf16[128,2048]{1,0:T(8,128)(2,1)} fusion(bf16[1,176,2048]{2,1,0:T(8,128)(2,1)S(1)} %copy-done.4, f32[128,176]{0,1:T(8,128)} %copy-done.7, f32[128,176]{0,1:T(8,128)S(1)} %fusion.43), kind=kOutput, calls=%fused_computation.33 | convolution fusion | flops 92672000 | bytes 1425408 | tf_op jit(solution)/shard_map/dot_general | solution.py:62
  36.3 1.2 %fusion.33 = (f32[8]{0:T(128)S(1)}, f32[8]{0:T(128)S(1)}, f32[8]{0:T(128)S(1)}, f32[8]{0:T(128)S(1)}) fusion(bf16[1,8,37984]{2,1,0:T(8,128)(2,1)S(1)} %collective-permute-done.3, bf16[1,8,37984]{2,1,0:T(8,128)(2,1)S(1)} %copy-done.1, f32[8]{0:T(128)S(1)} %reduce_max.45, s32[8]{0:T(128)S(1)} %bitcast.142, s32[37984]{0:T(1024)S(1)} %iota_add_fusion, ...), kind=kLoop, calls=%fused_computation.56 | loop fusion | flops 3646432 | bytes 1367648 | tf_op jit(solution)/shard_map/reduce_sum | solution.py:110
  38.3 7.3 %all-reduce.6 = (f32[32]{0:T(128)S(1)}, f32[32]{0:T(128)S(1)}, f32[32]{0:T(128)S(1)}, f32[32]{0:T(128)S(1)}, f32[32]{0:T(128)S(1)}, /*index=5*/f32[32]{0:T(128)S(1)}) all-reduce(f32[32]{0:T(128)S(1)} %convert_dynamic-update-slice_fusion.1, f32[32]{0:T(128)S(1)} %dynamic-update-slice.1, ...), channel_id=2, replica_groups=mesh['peer'=8,'grp'=4] {'grp'}, use_global_device_ids=true, to_apply=%add | all-reduce | flops 192 | bytes 1536
  46.4 0.5 subtract_bitcast_fusion
  47.0 3.7 %all-to-all-start.1 = ((bf16[4,2,16,2048]{3,2,1,0:T(8,128)(2,1)}), bf16[4,2,16,2048]{3,2,1,0:T(8,128)(2,1)S(1)}, u32[]{:S(2)}, u32[]{:S(2)}) async-start(bf16[4,2,16,2048]{3,2,1,0:T(8,128)(2,1)} %bitcast.130), calls=%async_computation.1 | async-start | bytes 1048576 | tf_op jit(solution)/shard_map/all_to_all | solution.py:172
  50.6 1.4 %fusion.29 = bf16[1,8,37984]{2,1,0:T(8,128)(2,1)} fusion(bf16[1,8,37984]{2,1,0:T(8,128)(2,1)S(1)} %copy-done.1, bf16[1,8,37984]{2,1,0:T(8,128)(2,1)S(1)} %collective-permute-done.3, f32[8]{0:T(128)S(1)} %get-tuple-element.380, s32[37984]{0:T(1024)S(1)} %iota_add_fusion, f32[8]{0:T(128)S(1)} %get-tuple-element.379, s32[8]{0:T(128)S(1)} %bitcast.143), kind=kLoop, calls=%fused_computation.52 | loop fusion | flops 3038720 | bytes 1975264 | tf_op jit(solution)/shard_map/convert_element_type | solution.py:122
  52.1 3.6 %gather_fusion.2 = f32[512,2048]{1,0:T(8,128)} fusion(f32[32,2048]{1,0:T(8,128)S(1)} %bitcast.126, s32[1024]{0:T(1024)S(1)} %pad_clamp_fusion), kind=kCustom, calls=%fused_computation.1.clone | custom fusion | bytes 8390656 | tf_op jit(solution)/shard_map/jit(_take)/gather | solution.py:192
  55.8 5.2 %reshape.357 = f32[128,4,2048]{2,1,0:T(4,128)} reshape(f32[512,2048]{1,0:T(8,128)} %gather_fusion.2) | data formatting | bytes 8388608 | tf_op jit(solution)/shard_map/jit(_take)/gather | solution.py:192
  61.0 3.6 %gather_fusion.1 = f32[512,2048]{1,0:T(8,128)} fusion(f32[32,2048]{1,0:T(8,128)S(1)} %bitcast.125, s32[1024]{0:T(1024)S(1)} %pad_clamp_fusion), kind=kCustom, calls=%fused_computation.clone | custom fusion | bytes 8390656 | tf_op jit(solution)/shard_map/jit(_take)/gather | solution.py:187
  64.6 5.3 %reshape.353 = f32[128,4,2048]{2,1,0:T(4,128)} reshape(f32[512,2048]{1,0:T(8,128)} %gather_fusion.1) | data formatting | bytes 8388608 | tf_op jit(solution)/shard_map/jit(_take)/gather | solution.py:187
  69.8 11.4 %multiply_reduce_fusion = (f32[128,4]{1,0:T(8,128)S(1)}, bf16[128,2048]{1,0:T(8,128)(2,1)}, bf16[128,2048]{1,0:T(8,128)(2,1)}) fusion(f32[128,4,2048]{2,1,0:T(4,128)} %reshape.353, f32[128,2048]{1,0:T(8,128)S(1)} %copy-done.2, pred[128,4]{1,0:T(8,128)(4,1)S(1)} %copy.46, pred[128,4]{1,0:T(8,128)(4,1)S(1)} %copy.41, f32[128,4]{1,0:T(8,128)S(1)} %copy-done.9, ...), kind=kLoop, calls=%fused_computation.29 | loop fusion | flops 8912384 | bytes 10490880 | tf_op jit(solution)/shard_map/reduce_sum | solution.py:196
  81.2 0.7 copy.50
  (94 shorter events, 5.6 us)
Async XLA Ops:
  0.6 26.5 %copy-start = (bf16[1,2048,176]{1,2,0:T(8,128)(2,1)S(1)}, bf16[1,2048,176]{1,2,0:T(8,128)(2,1)}, u32[]{:S(2)}) copy-start(bf16[1,2048,176]{1,2,0:T(8,128)(2,1)} %param.18) | copy-start | bytes 2162692
  0.6 8.7 %copy-start.8 = (bf16[128,2048]{1,0:T(8,128)(2,1)S(1)}, bf16[128,2048]{1,0:T(8,128)(2,1)}, u32[]{:S(2)}) copy-start(bf16[128,2048]{1,0:T(8,128)(2,1)} %param.14) | copy-start | bytes 1572868
  3.3 10.6 %copy-start.10 = (s32[128,4]{0,1:T(4,128)S(1)}, s32[128,4]{0,1:T(4,128)}, u32[]{:S(2)}) copy-start(s32[128,4]{0,1:T(4,128)} %param.16) | copy-start | bytes 6148
  3.3 18.7 %collective-permute-start = (bf16[1,1,2,16,2048]{4,3,2,1,0:T(8,128)(2,1)S(1)}, bf16[1,1,2,16,2048]{4,3,2,1,0:T(8,128)(2,1)}, u32[]{:S(2)}, u32[]{:S(2)}) collective-permute-start(bf16[1,1,2,16,2048]{4,3,2,1,0:T(8,128)(2,1)S(1)} %bitcast.132), channel_id=1, source_target_pairs={{0,1},{1,2},{2,3},{3,0},{4,5},{5,6},{6,7},{7,4},{8,9},{9,10},{10,1... | collective-permute-start | bytes 393224 | tf_op jit(solution)/shard_map/ppermute | solution.py:28
  3.9 19.2 %collective-permute-start.1 = (bf16[1,1,2,16,2048]{4,3,2,1,0:T(8,128)(2,1)S(1)}, bf16[1,1,2,16,2048]{4,3,2,1,0:T(8,128)(2,1)}, u32[]{:S(2)}, u32[]{:S(2)}) collective-permute-start(bf16[1,1,2,16,2048]{4,3,2,1,0:T(8,128)(2,1)S(1)} %bitcast.133), channel_id=1, source_target_pairs={{0,2},{1,3},{2,0},{3,1},{4,6},{5,7},{6,4},{7,5},{8,10},{9,11},{10,... | collective-permute-start | bytes 393224 | tf_op jit(solution)/shard_map/ppermute | solution.py:28
  6.4 17.6 %collective-permute-start.2 = (bf16[1,1,2,16,2048]{4,3,2,1,0:T(8,128)(2,1)S(1)}, bf16[1,1,2,16,2048]{4,3,2,1,0:T(8,128)(2,1)}, u32[]{:S(2)}, u32[]{:S(2)}) collective-permute-start(bf16[1,1,2,16,2048]{4,3,2,1,0:T(8,128)(2,1)S(1)} %bitcast.134), channel_id=1, source_target_pairs={{0,3},{1,0},{2,1},{3,2},{4,7},{5,4},{6,5},{7,6},{8,11},{9,8},{10,9... | collective-permute-start | bytes 393224 | tf_op jit(solution)/shard_map/ppermute | solution.py:28
  7.8 27.9 %collective-permute-start.3 = (bf16[1,8,37984]{2,1,0:T(8,128)(2,1)}, bf16[1,8,37984]{2,1,0:T(8,128)(2,1)S(1)}, u32[]{:S(2)}, u32[]{:S(2)}) collective-permute-start(bf16[1,8,37984]{2,1,0:T(8,128)(2,1)} %param.22), channel_id=1, source_target_pairs={{0,4},{4,8},{8,12},{12,16},{16,20},{20,24},{24,28},{28,0},{1,5},{5... | collective-permute-start | bytes 1823240 | tf_op jit(solution)/shard_map/ppermute | solution.py:46
  10.4 16.7 %all-to-all-start = ((bf16[4,2,16,2048]{3,2,1,0:T(8,128)(2,1)}), bf16[4,2,16,2048]{3,2,1,0:T(8,128)(2,1)S(1)}, u32[]{:S(2)}, u32[]{:S(2)}) async-start(bf16[4,2,16,2048]{3,2,1,0:T(8,128)(2,1)} %broadcast_in_dim.65), calls=%async_computation | async-start | bytes 1048576 | tf_op jit(solution)/shard_map/all_to_all | solution.py:163
  14.1 3.7 %copy-start.1 = (bf16[1,8,37984]{2,1,0:T(8,128)(2,1)S(1)}, bf16[1,8,37984]{2,1,0:T(8,128)(2,1)}, u32[]{:S(2)}) copy-start(bf16[1,8,37984]{2,1,0:T(8,128)(2,1)} %param.21) | copy-start | bytes 1823236
  14.1 4.1 %copy-start.13 = (u32[32]{0:T(128)S(1)}, u32[32]{0:T(128)}, u32[]{:S(2)}) copy-start(u32[32]{0:T(128)} %constant.149) | copy-start | bytes 388
  14.2 5.5 %copy-start.5 = (bf16[128,2048]{1,0:T(8,128)(2,1)S(1)}, bf16[128,2048]{1,0:T(8,128)(2,1)}, u32[]{:S(2)}) copy-start(bf16[128,2048]{1,0:T(8,128)(2,1)} %param.15) | copy-start | bytes 1572868
  17.6 3.2 %copy-start.11 = (f32[128,4]{0,1:T(4,128)S(1)}, f32[128,4]{0,1:T(4,128)}, u32[]{:S(2)}) copy-start(f32[128,4]{0,1:T(4,128)} %param.17) | copy-start | bytes 6148
  24.9 2.6 %copy-start.3 = (bf16[1,2048,176]{1,2,0:T(8,128)(2,1)S(1)}, bf16[1,2048,176]{1,2,0:T(8,128)(2,1)}, u32[]{:S(2)}) copy-start(bf16[1,2048,176]{1,2,0:T(8,128)(2,1)} %param.19) | copy-start | bytes 2162692
  27.1 1.5 %copy-start.6 = (f32[128,176]{0,1:T(8,128)S(1)}, f32[128,176]{0,1:T(8,128)}, u32[]{:S(2)}) copy-start(f32[128,176]{0,1:T(8,128)} %fusion.35) | copy-start | bytes 270340
  27.9 0.6 copy-start.7
  30.1 3.6 %copy-start.4 = (bf16[1,176,2048]{2,1,0:T(8,128)(2,1)S(1)}, bf16[1,176,2048]{2,1,0:T(8,128)(2,1)}, u32[]{:S(2)}) copy-start(bf16[1,176,2048]{2,1,0:T(8,128)(2,1)} %param.20) | copy-start | bytes 2162692
  30.1 16.9 %all-to-all-start.2 = ((bf16[4,2,16,2048]{3,2,1,0:T(8,128)(2,1)}), bf16[4,2,16,2048]{3,2,1,0:T(8,128)(2,1)S(1)}, u32[]{:S(2)}, u32[]{:S(2)}) async-start(bf16[4,2,16,2048]{3,2,1,0:T(8,128)(2,1)} %bitcast.20), calls=%async_computation.2 | async-start | bytes 1048576 | tf_op jit(solution)/shard_map/all_to_all | solution.py:173
  33.7 2.6 %copy-start.12 = (s32[1,8]{1,0:T(1,128)S(1)}, s32[1,8]{1,0:T(1,128)}, u32[]{:S(2)}) copy-start(s32[1,8]{1,0:T(1,128)} %param.23) | copy-start | bytes 100
  47.0 14.0 %all-to-all-start.1 = ((bf16[4,2,16,2048]{3,2,1,0:T(8,128)(2,1)}), bf16[4,2,16,2048]{3,2,1,0:T(8,128)(2,1)S(1)}, u32[]{:S(2)}, u32[]{:S(2)}) async-start(bf16[4,2,16,2048]{3,2,1,0:T(8,128)(2,1)} %bitcast.130), calls=%async_computation.1 | async-start | bytes 1048576 | tf_op jit(solution)/shard_map/all_to_all | solution.py:172
  64.6 5.3 %copy-start.2 = (f32[128,2048]{1,0:T(8,128)S(1)}, f32[128,2048]{1,0:T(8,128)}, u32[]{:S(2)}) copy-start(f32[128,2048]{1,0:T(8,128)} %convert_element_type.89) | copy-start | bytes 3145732
  64.6 5.3 %copy-start.9 = (f32[128,4]{1,0:T(8,128)S(1)}, f32[128,4]{1,0:T(8,128)}, u32[]{:S(2)}) copy-start(f32[128,4]{1,0:T(8,128)} %copy.40) | copy-start | bytes 6148
